TPU v7x, 32 devices: a whole 2x2x4 slice. The times are simulated.
32 devices in a mesh: row: 4 (over z), col: 8 (over y, x, core).
Axes of the slice: x: 2, y: 2, z: 4, core: 2. Of those that a mesh axis runs over, the one named last changes fastest.
Arguments:
- image: float32 [16, 16, 64, 128], P('row', 'col'), may hold values from -6 to 6
- u_factors: bfloat16 [20, 16, 1024, 256], P('row', 'col'), may hold values from -0.125 to 0.125
- v_factors: bfloat16 [20, 16, 1024, 256], P('row', 'col'), may hold values from -0.1875 to 0.1875
- ranks: int32 [20, 16], P('row', 'col'), may hold values from 16 to 256
- measured: bfloat16 [20480, 128], P('row'), may hold values from -6 to 6
Outputs:
- new_image: float32 [16, 16, 64, 128], P('row', 'col')
All inputs are finite; a program needn't handle non-finite values.
Results may differ from a plain program's by a relative error of at most 0.0051.
Values may be sent and summed in bfloat16 or wider, within the bound.
No kernel may reach another device: no remote copies, remote signals or barrier semaphores. Data moves between devices by JAX's collectives and lax.ppermute only.
A program may use at most 128 MiB of HBM per device.

v0:
```python
import jax
import jax.numpy as jnp
from jax import lax
from jax.sharding import PartitionSpec as P

diff_rate = 0.12
edge_scale = 0.5


def padded_2(block, sides, width):
    for axis, dim in sides:
        count = lax.axis_size(axis)
        forward = [(i, i + 1) for i in range(count - 1)]
        backward = [(target, source) for source, target in forward]
        low = lax.ppermute(
            lax.slice_in_dim(block, block.shape[dim] - width, None, axis=dim), axis, forward
        )
        high = lax.ppermute(lax.slice_in_dim(block, 0, width, axis=dim), axis, backward)
        block = jnp.concatenate([low, block, high], axis=dim)
    return block


def flux(delta):
    scaled = delta / edge_scale
    return delta / (1.0 + scaled * scaled)


def diffuse_margin(extended):
    padded = jnp.pad(extended, ((0, 0), (0, 0), (1, 1), (0, 0)))
    center = padded[1:-1, 1:-1, 1:-1]
    total = flux(padded[2:, 1:-1, 1:-1] - center) + flux(padded[:-2, 1:-1, 1:-1] - center)
    total = total + flux(padded[1:-1, 2:, 1:-1] - center) + flux(padded[1:-1, :-2, 1:-1] - center)
    total = total + flux(padded[1:-1, 1:-1, 2:] - center) + flux(padded[1:-1, 1:-1, :-2] - center)
    return center + diff_rate * total


def body(image, u_factors, v_factors, ranks, measured):
    row_tiles, col_tiles, tile_len, rank_max = u_factors.shape
    frames = image.shape[3]
    local_x, local_y = (image.shape[0], image.shape[1])
    whole = lax.all_gather(image.astype(jnp.bfloat16), "row", axis=0, tiled=True)
    xtiles = whole.reshape(col_tiles, tile_len, frames)
    levels = lax.broadcasted_iota(jnp.int32, (row_tiles, col_tiles, rank_max), 2)
    mask = (levels < ranks[:, :, None]).astype(jnp.float32)
    coef = jnp.einsum("ijkr,jkf->ijrf", v_factors, xtiles, preferred_element_type=jnp.float32)
    coef = (coef * mask[:, :, :, None]).astype(jnp.bfloat16)
    partial_value = jnp.einsum(
        "ijkr,ijrf->ikf", u_factors, coef, preferred_element_type=jnp.float32
    )
    partial_value = partial_value.reshape(row_tiles * tile_len, frames)
    total = lax.psum(partial_value, "col")
    resid = (total - measured.astype(jnp.float32)).astype(jnp.bfloat16)
    resid = resid.reshape(row_tiles, tile_len, frames)
    back = jnp.einsum("ijkr,ikf->ijrf", u_factors, resid, preferred_element_type=jnp.float32)
    back = (back * mask[:, :, :, None]).astype(jnp.bfloat16)
    grad_terms = jnp.einsum("ijkr,ijrf->jkf", v_factors, back, preferred_element_type=jnp.float32)
    grad_terms = grad_terms.reshape(col_tiles * tile_len, frames)
    gradient = lax.psum_scatter(grad_terms, "row", scatter_dimension=0, tiled=True)
    moved = image - gradient.reshape(image.shape)
    extended = padded_2(moved, (("row", 0), ("col", 1)), 2)
    middle = diffuse_margin(extended)
    grid_x = local_x * lax.axis_size("row")
    grid_y = local_y * lax.axis_size("col")
    pos_x = (
        lax.broadcasted_iota(jnp.int32, (local_x + 2, 1, 1, 1), 0)
        + lax.axis_index("row") * local_x
        - 1
    )
    pos_y = (
        lax.broadcasted_iota(jnp.int32, (1, local_y + 2, 1, 1), 1)
        + lax.axis_index("col") * local_y
        - 1
    )
    inside = (pos_x >= 0) & (pos_x < grid_x) & ((pos_y >= 0) & (pos_y < grid_y))
    middle = jnp.where(inside, middle, 0.0)
    moved = diffuse_margin(middle)
    return moved


def solution(mesh):
    placed = (
        P("row", "col", None, None),
        P("row", "col", None, None),
        P("row", "col", None, None),
        P("row", "col"),
        P("row", None),
    )
    return jax.shard_map(
        body, mesh=mesh, in_specs=placed, out_specs=P("row", "col", None, None), check_vma=False
    )
```

profile of v0, /device:TPU:1, one launch (start us, length us, event | category | flops | bytes accessed | tf_op | source)
XLA Modules:
  0.0 176.0 jit_solution(7555312063323355615)
XLA Ops:
  6.5 0.0 all-reduce.4.cloned.1.call-start
  6.5 0.8 copy.20
  7.3 0.1 compare_convert_fusion
  7.4 1.0 convert_element_type.29
  8.4 15.3 %all_gather.3 = bf16[16,2,64,128]{3,2,1,0:T(8,128)(2,1)S(1)} all-gather(bf16[4,2,64,128]{3,2,1,0:T(8,128)(2,1)S(1)} %convert_element_type.29), channel_id=1, replica_groups=mesh['row'=4,'col'=8] {'row'}, dimensions={0}, use_global_device_ids=true | all-gather | bytes 655360 | tf_op jit(solution)/shard_map/all_gather | solution.py:41
  23.7 6.6 %convolution_bitcast_fusion = f32[5,1024,128]{1,2,0:T(8,128)S(1)} fusion(bf16[5,2,1024,256]{3,2,1,0:T(8,128)(2,1)} %param.6, bf16[2,1024,128,1]{2,1,0,3:T(8,128)(2,1)S(1)} %bitcast.37, bf16[5,2,1024,256]{3,2,1,0:T(8,128)(2,1)} %param.7, f32[5,2,256]{2,1,0:T(2,128)S(1)} %compare_convert_fusion), kind=kOutput, calls=%fused_computation.7 | convolution fusion | flops 1342832640 | bytes 13641728 | tf_op jit(solution)/shard_map/ijkr,ijrf->ikf/dot_general | solution.py:47
  30.3 2.1 %copy.21 = f32[5,1024,128]{2,1,0:T(8,128)} copy(f32[5,1024,128]{1,2,0:T(8,128)S(1)} %convolution_bitcast_fusion) | data formatting | bytes 5242880 | tf_op jit(solution)/shard_map/ijkr,ijrf->ikf/dot_general | solution.py:47
  32.4 0.0 copy-start
  32.4 0.0 all-reduce.4.cloned.1.call-update
  32.4 0.0 reduce-scatter.2.cloned.1.call-start
  32.5 67.2 %all-reduce.4.cloned.1.call-done = f32[5120,128]{1,0:T(8,128)} async-done(((f32[5120,128]{1,0:T(8,128)}), f32[5120,128]{1,0:T(8,128)}) %all-reduce.4.cloned.1.call-update) | async-done | bytes 2621456 | tf_op jit(solution)/shard_map/psum | solution.py:51
  99.7 0.0 copy-done
  99.7 2.0 %subtract_convert_fusion = bf16[5120,128]{1,0:T(8,128)(2,1)S(1)} fusion(f32[5120,128]{1,0:T(8,128)} %all-reduce.4.cloned.1.call-done, bf16[5120,128]{1,0:T(8,128)(2,1)S(1)} %copy-done), kind=kLoop, calls=%fused_computation.4 | loop fusion | flops 1966080 | bytes 5242880 | tf_op jit(solution)/shard_map/convert_element_type | solution.py:52
  101.7 7.7 %fusion.8 = f32[2,1024,128]{1,2,0:T(8,128)} fusion(bf16[5,2,1024,256]{3,2,1,0:T(8,128)(2,1)} %param.7, bf16[5,1024,128,1]{2,1,0,3:T(8,128)(2,1)S(1)} %bitcast.38, bf16[5,2,1024,256]{3,2,1,0:T(8,128)(2,1)} %param.6, f32[5,2,256]{2,0,1:T(8,128)S(1)} %copy.24), kind=kOutput, calls=%fused_computation.12 | convolution fusion | flops 1342832640 | bytes 12855296 | tf_op jit(solution)/shard_map/ijkr,ijrf->jkf/dot_general | solution.py:56
  109.4 0.0 copy-start.1
  109.4 2.6 %copy.26 = f32[2,1024,128]{2,1,0:T(8,128)} copy(f32[2,1024,128]{1,2,0:T(8,128)} %fusion.8) | data formatting | bytes 2097152 | tf_op jit(solution)/shard_map/ijkr,ijrf->jkf/dot_general | solution.py:56
  112.0 0.0 reduce-scatter.2.cloned.1.call-update
  112.0 27.3 %reduce-scatter.2.cloned.1.call-done = f32[512,128]{1,0:T(8,128)} async-done(((f32[2048,128]{1,0:T(8,128)}), f32[512,128]{1,0:T(8,128)}) %reduce-scatter.2.cloned.1.call-update) | async-done | bytes 262160 | tf_op jit(solution)/shard_map/reduce_scatter | solution.py:58
  139.3 0.0 copy-done.1
  139.3 1.0 sub.51
  140.3 1.3 collective-permute-start
  141.6 1.3 collective-permute-start.1
  142.9 0.6 collective-permute-done
  143.5 4.7 %collective-permute-done.1 = f32[2,2,64,128]{3,2,1,0:T(8,128)S(1)} collective-permute-done((f32[2,2,64,128]{3,2,1,0:T(8,128)S(1)}, f32[2,2,64,128]{3,2,1,0:T(8,128)S(1)}, u32[]{:S(2)}, u32[]{:S(2)}) %collective-permute-start.1) | collective-permute-done | bytes 131104 | tf_op jit(solution)/shard_map/ppermute | solution.py:18
  148.2 4.6 %collective-permute-start.2 = (f32[8,2,64,128]{3,2,1,0:T(8,128)S(1)}, f32[8,2,64,128]{3,2,1,0:T(8,128)S(1)}, u32[]{:S(2)}, u32[]{:S(2)}) collective-permute-start(f32[8,2,64,128]{3,2,1,0:T(8,128)S(1)} %pad_maximum_fusion.7), channel_id=1, source_target_pairs={{0,1},{1,2},{2,3},{3,4},{4,5},{5,6},{6,7},{8,9},{9,10},{10,11},{11... | collective-permute-start | bytes 1572872 | tf_op jit(solution)/shard_map/ppermute | solution.py:15
  152.9 1.9 %collective-permute-start.3 = (f32[8,2,64,128]{3,2,1,0:T(8,128)S(1)}, f32[8,2,64,128]{3,2,1,0:T(8,128)S(1)}, u32[]{:S(2)}, u32[]{:S(2)}) collective-permute-start(f32[8,2,64,128]{3,2,1,0:T(8,128)S(1)} %pad_maximum_fusion.7), channel_id=1, source_target_pairs={{1,0},{2,1},{3,2},{4,3},{5,4},{6,5},{7,6},{9,8},{10,9},{11,10},{12... | collective-permute-start | bytes 1572872 | tf_op jit(solution)/shard_map/ppermute | solution.py:18
  154.8 0.1 broadcast_and_fusion
  154.9 4.1 %collective-permute-done.2 = f32[8,2,64,128]{3,2,1,0:T(8,128)S(1)} collective-permute-done((f32[8,2,64,128]{3,2,1,0:T(8,128)S(1)}, f32[8,2,64,128]{3,2,1,0:T(8,128)S(1)}, u32[]{:S(2)}, u32[]{:S(2)}) %collective-permute-start.2) | collective-permute-done | bytes 524320 | tf_op jit(solution)/shard_map/ppermute | solution.py:15
  159.0 7.2 %collective-permute-done.3 = f32[8,2,64,128]{3,2,1,0:T(8,128)S(1)} collective-permute-done((f32[8,2,64,128]{3,2,1,0:T(8,128)S(1)}, f32[8,2,64,128]{3,2,1,0:T(8,128)S(1)}, u32[]{:S(2)}, u32[]{:S(2)}) %collective-permute-start.3) | collective-permute-done | bytes 524320 | tf_op jit(solution)/shard_map/ppermute | solution.py:18
  166.2 0.2 pad_maximum_fusion
  166.4 1.6 add_select_fusion
  168.0 1.1 multiply_add_fusion
  (5 shorter events, 0.1 us)
Async XLA Ops:
  6.5 93.1 %all-reduce.4.cloned.1.call-start = ((), (), s32[]{:S(2)}) async-start(), calls=%async_computation.1 | async-start | bytes 5242880 | tf_op jit(solution)/shard_map/psum | solution.py:51
  32.4 67.3 %copy-start = (bf16[5120,128]{1,0:T(8,128)(2,1)S(1)}, bf16[5120,128]{1,0:T(8,128)(2,1)}, u32[]{:S(2)}) copy-start(bf16[5120,128]{1,0:T(8,128)(2,1)} %param.9) | copy-start | bytes 3932164
  32.4 106.8 %reduce-scatter.2.cloned.1.call-start = ((), (), s32[]{:S(2)}) async-start(), calls=%async_computation.2 | async-start | bytes 1310720 | tf_op jit(solution)/shard_map/reduce_scatter | solution.py:58
  109.4 29.9 %copy-start.1 = (f32[4,2,64,128]{3,2,1,0:T(8,128)S(1)}, f32[4,2,64,128]{3,2,1,0:T(8,128)}, u32[]{:S(2)}) copy-start(f32[4,2,64,128]{3,2,1,0:T(8,128)} %param.5) | copy-start | bytes 786436
  140.3 3.2 %collective-permute-start = (f32[2,2,64,128]{3,2,1,0:T(8,128)S(1)}, f32[2,2,64,128]{3,2,1,0:T(8,128)S(1)}, u32[]{:S(2)}, u32[]{:S(2)}) collective-permute-start(f32[2,2,64,128]{3,2,1,0:T(8,128)S(1)} %get-tuple-element.5), channel_id=1, source_target_pairs={{0,8},{8,16},{16,24},{1,9},{9,17},{17,25},{2,10},{10,18},{18,26},{... | collective-permute-start | bytes 393224 | tf_op jit(solution)/shard_map/ppermute | solution.py:15
  141.6 6.6 %collective-permute-start.1 = (f32[2,2,64,128]{3,2,1,0:T(8,128)S(1)}, f32[2,2,64,128]{3,2,1,0:T(8,128)S(1)}, u32[]{:S(2)}, u32[]{:S(2)}) collective-permute-start(f32[2,2,64,128]{3,2,1,0:T(8,128)S(1)} %get-tuple-element.6), channel_id=1, source_target_pairs={{8,0},{16,8},{24,16},{9,1},{17,9},{25,17},{10,2},{18,10},{26,18},{... | collective-permute-start | bytes 393224 | tf_op jit(solution)/shard_map/ppermute | solution.py:18
  148.2 10.7 %collective-permute-start.2 = (f32[8,2,64,128]{3,2,1,0:T(8,128)S(1)}, f32[8,2,64,128]{3,2,1,0:T(8,128)S(1)}, u32[]{:S(2)}, u32[]{:S(2)}) collective-permute-start(f32[8,2,64,128]{3,2,1,0:T(8,128)S(1)} %pad_maximum_fusion.7), channel_id=1, source_target_pairs={{0,1},{1,2},{2,3},{3,4},{4,5},{5,6},{6,7},{8,9},{9,10},{10,11},{11... | collective-permute-start | bytes 1572872 | tf_op jit(solution)/shard_map/ppermute | solution.py:15
  152.9 13.3 %collective-permute-start.3 = (f32[8,2,64,128]{3,2,1,0:T(8,128)S(1)}, f32[8,2,64,128]{3,2,1,0:T(8,128)S(1)}, u32[]{:S(2)}, u32[]{:S(2)}) collective-permute-start(f32[8,2,64,128]{3,2,1,0:T(8,128)S(1)} %pad_maximum_fusion.7), channel_id=1, source_target_pairs={{1,0},{2,1},{3,2},{4,3},{5,4},{6,5},{7,6},{9,8},{10,9},{11,10},{12... | collective-permute-start | bytes 1572872 | tf_op jit(solution)/shard_map/ppermute | solution.py:18
Sparse Core Ops, SparseCore 0:
  32.6 67.0 all-reduce.3
  112.1 27.1 reduce-scatter.1
where the time goes:
time: 176 us
  waiting for transfers between devices  111 us (63%)
  blocking collectives  15.3 us (9%)
  matrix products  14.3 us (8%)
  between operations  13.5 us (8%)
  starting transfers between devices  9.15 us (5%)
  other arithmetic  7.07 us (4%)
  local copies, waits for them, and re-layouts  5.47 us (3%)
    psum x1, waiting for transfers between devices, body(): total = lax.psum(partial_value, 'col')  67.2 us
    reduce_scatter x1, waiting for transfers between devices, body(): lax.psum_scatter(grad_terms, 'row', scatter_dimension=0, tiled=True)  27.3 us
    all_gather x1, blocking collectives, body(): lax.all_gather(image.astype(jnp.bfloat16), 'row', axis=0, tiled=True)  15.3 us
    ppermute x2, waiting for transfers between devices, padded_2(): lax.ppermute(lax.slice_in_dim(block, 0, width, axis=dim), axis, backward)  11.9 us
    dot_general x1, matrix products, body(): jnp.einsum('ijkr,ijrf->jkf', v_factors, back, preferred_element_type=jnp....  7.72 us
    dot_general x1, matrix products, body(): jnp.einsum('ijkr,ijrf->ikf', u_factors, coef, preferred_element_type=jnp....  6.62 us
    ppermute x2, starting transfers between devices, padded_2(): lax.ppermute(lax.slice_in_dim(block, block.shape[dim] - width, None, axis...  5.9 us
    ppermute x2, waiting for transfers between devices, padded_2(): lax.ppermute(lax.slice_in_dim(block, block.shape[dim] - width, None, axis...  4.69 us
  transfers between devices with their start and end apart: 6, of which 6 were waited for; matrix products, arithmetic and copies ran while one was open for 0% of the time, Pallas kernels for 0%

commit v1 on v0

--- a/solution.py
+++ b/solution.py
@@ -38,7 +38,19 @@
     row_tiles, col_tiles, tile_len, rank_max = u_factors.shape
     frames = image.shape[3]
     local_x, local_y = (image.shape[0], image.shape[1])
-    whole = lax.all_gather(image.astype(jnp.bfloat16), "row", axis=0, tiled=True)
+    x = image.astype(jnp.bfloat16)
+    ways, here, step = (lax.axis_size("row"), lax.axis_index("row"), x.shape[0])
+    dims = [n * ways if d == 0 else n for d, n in enumerate(x.shape)]
+    whole = lax.dynamic_update_slice_in_dim(jnp.zeros(dims, x.dtype), x, here * step, axis=0)
+    going_up = going_down = x
+    for far in range(1, ways // 2 + 1):
+        going_up = lax.ppermute(going_up, "row", [(d, (d + 1) % ways) for d in range(ways)])
+        whole = lax.dynamic_update_slice_in_dim(whole, going_up, (here - far) % ways * step, axis=0)
+        if 2 * far < ways:
+            going_down = lax.ppermute(going_down, "row", [(d, (d - 1) % ways) for d in range(ways)])
+            whole = lax.dynamic_update_slice_in_dim(
+                whole, going_down, (here + far) % ways * step, axis=0
+            )
     xtiles = whole.reshape(col_tiles, tile_len, frames)
     levels = lax.broadcasted_iota(jnp.int32, (row_tiles, col_tiles, rank_max), 2)
     mask = (levels < ranks[:, :, None]).astype(jnp.float32)

time: 176 us -> 171 us (0.972); the launches traced: 176 us -> 168 us
  blocking collectives: 15.3 us -> 0 us
  starting transfers between devices: 9.15 us -> 13.4 us
  waiting for transfers between devices: 111 us -> 114 us
    all_gather x1 -> x0, blocking collectives: 15.3 us -> none  [body(): lax.all_gather(image.astype(jnp.bfloat16), 'row', axis=0, tiled=True)]
    ppermute x0 -> x3, waiting for transfers between devices: none -> 7.93 us  [the longest x2 5.52 us: body(): lax.ppermute(going_up, 'row', [(d, (d + 1) % ways) for d in range(ways)])]
    ppermute x0 -> x3, starting transfers between devices: none -> 4.26 us  [the longest x2 2.17 us: body(): lax.ppermute(going_up, 'row', [(d, (d + 1) % ways) for d in range(ways)])]
    ppermute x2, waiting for transfers between devices: 4.69 us -> 0.63 us  [padded_2(): lax.ppermute(lax.slice_in_dim(block, block.shape[dim] - width, None, axis...]
  transfers between devices with their start and end apart: 6 -> 9, of which waited for: 6 -> 8; matrix products, arithmetic and copies ran while one was open for 0% -> 1% of each run, Pallas kernels for 0% -> 0%
where the time goes in v1:
time: 171 us; the launch traced here: 168 us
  waiting for transfers between devices  114 us (67%)
  matrix products  14.3 us (8%)
  between operations  13.5 us (8%)
  starting transfers between devices  13.4 us (8%)
  other arithmetic  7.79 us (5%)
  local copies, waits for them, and re-layouts  4.91 us (3%)
    psum x1, waiting for transfers between devices, body(): total = lax.psum(partial_value, 'col')  65.9 us
    reduce_scatter x1, waiting for transfers between devices, body(): lax.psum_scatter(grad_terms, 'row', scatter_dimension=0, tiled=True)  27.3 us
    ppermute x2, waiting for transfers between devices, padded_2(): lax.ppermute(lax.slice_in_dim(block, 0, width, axis=dim), axis, backward)  12.3 us
    dot_general x1, matrix products, body(): jnp.einsum('ijkr,ijrf->jkf', v_factors, back, preferred_element_type=jnp....  7.69 us
    dot_general x1, matrix products, body(): jnp.einsum('ijkr,ijrf->ikf', u_factors, coef, preferred_element_type=jnp....  6.62 us
    ppermute x2, waiting for transfers between devices, body(): lax.ppermute(going_up, 'row', [(d, (d + 1) % ways) for d in range(ways)])  5.52 us
    ppermute x2, starting transfers between devices, padded_2(): lax.ppermute(lax.slice_in_dim(block, 0, width, axis=dim), axis, backward)  4.79 us
    ppermute x2, starting transfers between devices, padded_2(): lax.ppermute(lax.slice_in_dim(block, block.shape[dim] - width, None, axis...  4.3 us
  transfers between devices with their start and end apart: 9, of which 8 were waited for; matrix products, arithmetic and copies ran while one was open for 1% of the time, Pallas kernels for 0%

profile of v1, /device:TPU:1, one launch (start us, length us, event | category | flops | bytes accessed | tf_op | source)
XLA Modules:
  0.0 168.1 jit_solution(2017379269655971587)
XLA Ops:
  6.5 0.0 all-reduce.4.cloned.1.call-start
  6.5 0.1 broadcast_in_dim.19
  6.7 1.0 constant_dynamic-update-slice_fusion.3
  7.7 2.2 %collective-permute-start = (bf16[4,2,64,128]{3,2,1,0:T(8,128)(2,1)S(1)}, bf16[4,2,64,128]{3,2,1,0:T(8,128)(2,1)S(1)}, u32[]{:S(2)}, u32[]{:S(2)}) collective-permute-start(bf16[4,2,64,128]{3,2,1,0:T(8,128)(2,1)S(1)} %get-tuple-element.6), channel_id=1, source_target_pairs={{0,8},{8,16},{16,24},{24,0},{1,9},{9,17},{17,25},{25,1},{2,10},{10... | collective-permute-start | bytes 393224 | tf_op jit(solution)/shard_map/ppermute | solution.py:47
  9.8 2.1 %collective-permute-start.1 = (bf16[4,2,64,128]{3,2,1,0:T(8,128)(2,1)S(1)}, bf16[4,2,64,128]{3,2,1,0:T(8,128)(2,1)S(1)}, u32[]{:S(2)}, u32[]{:S(2)}) collective-permute-start(bf16[4,2,64,128]{3,2,1,0:T(8,128)(2,1)S(1)} %get-tuple-element.6), channel_id=1, source_target_pairs={{0,24},{8,0},{16,8},{24,16},{1,25},{9,1},{17,9},{25,17},{2,26},{10... | collective-permute-start | bytes 393224 | tf_op jit(solution)/shard_map/ppermute | solution.py:50
  11.9 0.8 fusion.28
  12.7 2.4 %collective-permute-done = bf16[4,2,64,128]{3,2,1,0:T(8,128)(2,1)S(1)} collective-permute-done((bf16[4,2,64,128]{3,2,1,0:T(8,128)(2,1)S(1)}, bf16[4,2,64,128]{3,2,1,0:T(8,128)(2,1)S(1)}, u32[]{:S(2)}, u32[]{:S(2)}) %collective-permute-start) | collective-permute-done | bytes 131104 | tf_op jit(solution)/shard_map/ppermute | solution.py:47
  15.1 0.0 collective-permute-start.2
  15.1 2.4 %collective-permute-done.1 = bf16[4,2,64,128]{3,2,1,0:T(8,128)(2,1)S(1)} collective-permute-done((bf16[4,2,64,128]{3,2,1,0:T(8,128)(2,1)S(1)}, bf16[4,2,64,128]{3,2,1,0:T(8,128)(2,1)S(1)}, u32[]{:S(2)}, u32[]{:S(2)}) %collective-permute-start.1) | collective-permute-done | bytes 131104 | tf_op jit(solution)/shard_map/ppermute | solution.py:50
  17.5 3.2 %collective-permute-done.2 = bf16[4,2,64,128]{3,2,1,0:T(8,128)(2,1)S(1)} collective-permute-done((bf16[4,2,64,128]{3,2,1,0:T(8,128)(2,1)S(1)}, bf16[4,2,64,128]{3,2,1,0:T(8,128)(2,1)S(1)}, u32[]{:S(2)}, u32[]{:S(2)}) %collective-permute-start.2) | collective-permute-done | bytes 131104 | tf_op jit(solution)/shard_map/ppermute | solution.py:47
  20.7 6.6 %convolution_bitcast_fusion = f32[5,1024,128]{1,2,0:T(8,128)S(1)} fusion(bf16[5,2,1024,256]{3,2,1,0:T(8,128)(2,1)} %param.6, bf16[2,1024,128,1]{2,1,0,3:T(8,128)(2,1)S(1)} %bitcast.37, bf16[5,2,1024,256]{3,2,1,0:T(8,128)(2,1)} %param.7, f32[5,2,256]{2,1,0:T(2,128)S(1)} %copy.8), kind=kOutput, calls=%fused_computation.7 | convolution fusion | flops 1342832640 | bytes 13641728 | tf_op jit(solution)/shard_map/ijkr,ijrf->ikf/dot_general | solution.py:59
  27.3 2.1 %copy.9 = f32[5,1024,128]{2,1,0:T(8,128)} copy(f32[5,1024,128]{1,2,0:T(8,128)S(1)} %convolution_bitcast_fusion) | data formatting | bytes 5242880 | tf_op jit(solution)/shard_map/ijkr,ijrf->ikf/dot_general | solution.py:59
  29.5 0.0 copy-start
  29.5 0.0 all-reduce.4.cloned.1.call-update
  29.5 0.0 reduce-scatter.2.cloned.1.call-start
  29.6 65.9 %all-reduce.4.cloned.1.call-done = f32[5120,128]{1,0:T(8,128)} async-done(((f32[5120,128]{1,0:T(8,128)}), f32[5120,128]{1,0:T(8,128)}) %all-reduce.4.cloned.1.call-update) | async-done | bytes 2621456 | tf_op jit(solution)/shard_map/psum | solution.py:63
  95.5 0.0 copy-done
  95.5 2.0 %subtract_convert_fusion = bf16[5120,128]{1,0:T(8,128)(2,1)S(1)} fusion(f32[5120,128]{1,0:T(8,128)} %all-reduce.4.cloned.1.call-done, bf16[5120,128]{1,0:T(8,128)(2,1)S(1)} %copy-done), kind=kLoop, calls=%fused_computation.4 | loop fusion | flops 1966080 | bytes 5242880 | tf_op jit(solution)/shard_map/convert_element_type | solution.py:64
  97.5 7.7 %fusion.8 = f32[2,1024,128]{1,2,0:T(8,128)} fusion(bf16[5,2,1024,256]{3,2,1,0:T(8,128)(2,1)} %param.7, bf16[5,1024,128,1]{2,1,0,3:T(8,128)(2,1)S(1)} %bitcast.38, bf16[5,2,1024,256]{3,2,1,0:T(8,128)(2,1)} %param.6, f32[5,2,256]{2,0,1:T(8,128)S(1)} %fusion.28), kind=kOutput, calls=%fused_computation.12 | convolution fusion | flops 1342832640 | bytes 12855296 | tf_op jit(solution)/shard_map/ijkr,ijrf->jkf/dot_general | solution.py:68
  105.2 0.0 copy-start.1
  105.2 2.6 %copy.11 = f32[2,1024,128]{2,1,0:T(8,128)} copy(f32[2,1024,128]{1,2,0:T(8,128)} %fusion.8) | data formatting | bytes 2097152 | tf_op jit(solution)/shard_map/ijkr,ijrf->jkf/dot_general | solution.py:68
  107.7 0.0 reduce-scatter.2.cloned.1.call-update
  107.8 27.3 %reduce-scatter.2.cloned.1.call-done = f32[512,128]{1,0:T(8,128)} async-done(((f32[2048,128]{1,0:T(8,128)}), f32[512,128]{1,0:T(8,128)}) %reduce-scatter.2.cloned.1.call-update) | async-done | bytes 262160 | tf_op jit(solution)/shard_map/reduce_scatter | solution.py:70
  135.0 0.0 copy-done.1
  135.0 1.0 sub.59
  136.0 1.3 collective-permute-start.3
  137.3 1.3 collective-permute-start.4
  138.6 0.6 collective-permute-done.3
  139.3 4.7 %collective-permute-done.4 = f32[2,2,64,128]{3,2,1,0:T(8,128)S(1)} collective-permute-done((f32[2,2,64,128]{3,2,1,0:T(8,128)S(1)}, f32[2,2,64,128]{3,2,1,0:T(8,128)S(1)}, u32[]{:S(2)}, u32[]{:S(2)}) %collective-permute-start.4) | collective-permute-done | bytes 131104 | tf_op jit(solution)/shard_map/ppermute | solution.py:18
  144.0 3.5 %collective-permute-start.6 = (f32[8,2,64,128]{3,2,1,0:T(8,128)S(1)}, f32[8,2,64,128]{3,2,1,0:T(8,128)S(1)}, u32[]{:S(2)}, u32[]{:S(2)}) collective-permute-start(f32[8,2,64,128]{3,2,1,0:T(8,128)S(1)} %pad_maximum_fusion.7), channel_id=1, source_target_pairs={{1,0},{2,1},{3,2},{4,3},{5,4},{6,5},{7,6},{9,8},{10,9},{11,10},{12... | collective-permute-start | bytes 1572872 | tf_op jit(solution)/shard_map/ppermute | solution.py:18
  147.5 3.0 %collective-permute-start.5 = (f32[8,2,64,128]{3,2,1,0:T(8,128)S(1)}, f32[8,2,64,128]{3,2,1,0:T(8,128)S(1)}, u32[]{:S(2)}, u32[]{:S(2)}) collective-permute-start(f32[8,2,64,128]{3,2,1,0:T(8,128)S(1)} %pad_maximum_fusion.7), channel_id=1, source_target_pairs={{0,1},{1,2},{2,3},{3,4},{4,5},{5,6},{6,7},{8,9},{9,10},{10,11},{11... | collective-permute-start | bytes 1572872 | tf_op jit(solution)/shard_map/ppermute | solution.py:15
  150.6 0.1 broadcast_and_fusion
  150.7 7.6 %collective-permute-done.6 = f32[8,2,64,128]{3,2,1,0:T(8,128)S(1)} collective-permute-done((f32[8,2,64,128]{3,2,1,0:T(8,128)S(1)}, f32[8,2,64,128]{3,2,1,0:T(8,128)S(1)}, u32[]{:S(2)}, u32[]{:S(2)}) %collective-permute-start.6) | collective-permute-done | bytes 524320 | tf_op jit(solution)/shard_map/ppermute | solution.py:18
  158.3 0.0 collective-permute-done.5
  158.3 0.2 pad_maximum_fusion
  158.5 1.6 add_select_fusion
  160.1 1.1 multiply_add_fusion
  (8 shorter events, 0.1 us)
Async XLA Ops:
  6.5 88.9 %all-reduce.4.cloned.1.call-start = ((), (), s32[]{:S(2)}) async-start(), calls=%async_computation.1 | async-start | bytes 5242880 | tf_op jit(solution)/shard_map/psum | solution.py:63
  7.7 7.4 %collective-permute-start = (bf16[4,2,64,128]{3,2,1,0:T(8,128)(2,1)S(1)}, bf16[4,2,64,128]{3,2,1,0:T(8,128)(2,1)S(1)}, u32[]{:S(2)}, u32[]{:S(2)}) collective-permute-start(bf16[4,2,64,128]{3,2,1,0:T(8,128)(2,1)S(1)} %get-tuple-element.6), channel_id=1, source_target_pairs={{0,8},{8,16},{16,24},{24,0},{1,9},{9,17},{17,25},{25,1},{2,10},{10... | collective-permute-start | bytes 393224 | tf_op jit(solution)/shard_map/ppermute | solution.py:47
  9.8 7.7 %collective-permute-start.1 = (bf16[4,2,64,128]{3,2,1,0:T(8,128)(2,1)S(1)}, bf16[4,2,64,128]{3,2,1,0:T(8,128)(2,1)S(1)}, u32[]{:S(2)}, u32[]{:S(2)}) collective-permute-start(bf16[4,2,64,128]{3,2,1,0:T(8,128)(2,1)S(1)} %get-tuple-element.6), channel_id=1, source_target_pairs={{0,24},{8,0},{16,8},{24,16},{1,25},{9,1},{17,9},{25,17},{2,26},{10... | collective-permute-start | bytes 393224 | tf_op jit(solution)/shard_map/ppermute | solution.py:50
  15.1 5.6 %collective-permute-start.2 = (bf16[4,2,64,128]{3,2,1,0:T(8,128)(2,1)S(1)}, bf16[4,2,64,128]{3,2,1,0:T(8,128)(2,1)S(1)}, u32[]{:S(2)}, u32[]{:S(2)}) collective-permute-start(bf16[4,2,64,128]{3,2,1,0:T(8,128)(2,1)S(1)} %collective-permute-done), channel_id=1, source_target_pairs={{0,8},{8,16},{16,24},{24,0},{1,9},{9,17},{17,25},{25,1},{2,10},{10... | collective-permute-start | bytes 393224 | tf_op jit(solution)/shard_map/ppermute | solution.py:47
  29.5 66.0 %copy-start = (bf16[5120,128]{1,0:T(8,128)(2,1)S(1)}, bf16[5120,128]{1,0:T(8,128)(2,1)}, u32[]{:S(2)}) copy-start(bf16[5120,128]{1,0:T(8,128)(2,1)} %param.9) | copy-start | bytes 3932164
  29.5 105.5 %reduce-scatter.2.cloned.1.call-start = ((), (), s32[]{:S(2)}) async-start(), calls=%async_computation.2 | async-start | bytes 1310720 | tf_op jit(solution)/shard_map/reduce_scatter | solution.py:70
  105.2 29.9 %copy-start.1 = (f32[4,2,64,128]{3,2,1,0:T(8,128)S(1)}, f32[4,2,64,128]{3,2,1,0:T(8,128)}, u32[]{:S(2)}) copy-start(f32[4,2,64,128]{3,2,1,0:T(8,128)} %param.5) | copy-start | bytes 786436
  136.0 3.2 %collective-permute-start.3 = (f32[2,2,64,128]{3,2,1,0:T(8,128)S(1)}, f32[2,2,64,128]{3,2,1,0:T(8,128)S(1)}, u32[]{:S(2)}, u32[]{:S(2)}) collective-permute-start(f32[2,2,64,128]{3,2,1,0:T(8,128)S(1)} %get-tuple-element.7), channel_id=1, source_target_pairs={{0,8},{8,16},{16,24},{1,9},{9,17},{17,25},{2,10},{10,18},{18,26},{... | collective-permute-start | bytes 393224 | tf_op jit(solution)/shard_map/ppermute | solution.py:15
  137.3 6.6 %collective-permute-start.4 = (f32[2,2,64,128]{3,2,1,0:T(8,128)S(1)}, f32[2,2,64,128]{3,2,1,0:T(8,128)S(1)}, u32[]{:S(2)}, u32[]{:S(2)}) collective-permute-start(f32[2,2,64,128]{3,2,1,0:T(8,128)S(1)} %get-tuple-element.8), channel_id=1, source_target_pairs={{8,0},{16,8},{24,16},{9,1},{17,9},{25,17},{10,2},{18,10},{26,18},{... | collective-permute-start | bytes 393224 | tf_op jit(solution)/shard_map/ppermute | solution.py:18
  144.0 14.2 %collective-permute-start.6 = (f32[8,2,64,128]{3,2,1,0:T(8,128)S(1)}, f32[8,2,64,128]{3,2,1,0:T(8,128)S(1)}, u32[]{:S(2)}, u32[]{:S(2)}) collective-permute-start(f32[8,2,64,128]{3,2,1,0:T(8,128)S(1)} %pad_maximum_fusion.7), channel_id=1, source_target_pairs={{1,0},{2,1},{3,2},{4,3},{5,4},{6,5},{7,6},{9,8},{10,9},{11,10},{12... | collective-permute-start | bytes 1572872 | tf_op jit(solution)/shard_map/ppermute | solution.py:18
  147.5 10.7 %collective-permute-start.5 = (f32[8,2,64,128]{3,2,1,0:T(8,128)S(1)}, f32[8,2,64,128]{3,2,1,0:T(8,128)S(1)}, u32[]{:S(2)}, u32[]{:S(2)}) collective-permute-start(f32[8,2,64,128]{3,2,1,0:T(8,128)S(1)} %pad_maximum_fusion.7), channel_id=1, source_target_pairs={{0,1},{1,2},{2,3},{3,4},{4,5},{5,6},{6,7},{8,9},{9,10},{10,11},{11... | collective-permute-start | bytes 1572872 | tf_op jit(solution)/shard_map/ppermute | solution.py:15
Sparse Core Ops, SparseCore 0:
  29.6 65.7 all-reduce.3
  107.9 27.1 reduce-scatter.1
